TPU v7x, 512 devices: a whole 4x4x16 slice. The times are simulated.
512 devices in a mesh: row: 8 (over z_hi, core), col: 16 (over x, y), fsdp: 4 (over z_lo).
Axes of the slice: x: 4, y: 4, z: 16 (z_hi: 4, z_lo: 4; z = z_hi * 4 + z_lo), core: 2. Of those that a mesh axis runs over, the one named last changes fastest.
Arguments:
- layer_inputs: bfloat16 [4096, 8192], P('col', ('row', 'fsdp')), may hold values from -6 to 6
- output_grads: bfloat16 [4096, 14336], P(('row', 'fsdp'), 'col'), may hold values from -0.09375 to 0.09375
- weight: bfloat16 [8192, 14336], P(('row', 'fsdp'), 'col'), may hold values from -3 to 3
- moment: bfloat16 [8192, 14336], P(('row', 'fsdp'), 'col'), may hold values from -1.796875 to 1.796875
- variance: bfloat16 [8192, 14336], P(('row', 'fsdp'), 'col'), may hold values from 0.049804688 to 1
- keep_mask: int32 [64, 112], replicated, may hold values from 0 to 1, as said below
Outputs:
- new_weight: bfloat16 [8192, 14336], P(('row', 'fsdp'), 'col')
- new_moment: bfloat16 [8192, 14336], P(('row', 'fsdp'), 'col')
- new_variance: bfloat16 [8192, 14336], P(('row', 'fsdp'), 'col')
Inputs may be any that keep to these rules, and one draw needn't show every extreme that they name: `keep_mask`: 1 keeps a block of 128 x 128 weights, 0 drops it.
All inputs are finite; a program needn't handle non-finite values.
Results may differ from a plain program's by a relative error of at most 0.0039.
Values may be sent and summed in bfloat16 or wider, within the bound.
A program may use at most 128 MiB of HBM per device.

v0:
```python
import jax
import jax.numpy as jnp
from jax import lax
from jax.sharding import PartitionSpec as P

BS = 128
learn_rate = 0.02
beta_one = 0.9
beta_two = 0.95
epsilon = 1e-08
decay_rate = 0.1
first_fix = 1.0 - 0.9**10
second_fix = 1.0 - 0.95**10


def expand_keep(keep_tile):
    block_rows, block_cols = keep_tile.shape
    grid = jnp.broadcast_to(keep_tile[:, None, :, None], (block_rows, BS, block_cols, BS))
    return grid.reshape(block_rows * BS, block_cols * BS) > 0


def block_product(left_cols, right_cols):
    return lax.dot_general(
        left_cols, right_cols, (((0,), (0,)), ((), ())), preferred_element_type=jnp.float32
    )


def adam_update(grad, weight, moment, variance, keep_elem):
    weight_wide = weight.astype(jnp.float32)
    first = beta_one * moment.astype(jnp.float32) + (1.0 - beta_one) * grad
    second = beta_two * variance.astype(jnp.float32) + (1.0 - beta_two) * grad * grad
    direction = (
        first / first_fix / (jnp.sqrt(second / second_fix) + epsilon) + decay_rate * weight_wide
    )
    new_weight = jnp.where(
        keep_elem, (weight_wide - learn_rate * direction).astype(jnp.bfloat16), weight
    )
    new_moment = jnp.where(keep_elem, first.astype(jnp.bfloat16), moment)
    new_variance = jnp.where(keep_elem, second.astype(jnp.bfloat16), variance)
    return (new_weight, new_moment, new_variance)


def per_device(layer_inputs, output_grads, weight, moment, variance, keep_mask):
    fsdp_count = lax.axis_size("fsdp")
    rank_row = lax.axis_index("row")
    rank_col = lax.axis_index("col")
    rank_fsdp = lax.axis_index("fsdp")
    local_rows = weight.shape[0]
    local_cols = weight.shape[1]
    row_blocks = local_rows // BS
    col_blocks = local_cols // BS
    tile_keep = lax.dynamic_slice(
        keep_mask,
        ((rank_row * fsdp_count + rank_fsdp) * row_blocks, rank_col * col_blocks),
        (row_blocks, col_blocks),
    )
    grads_all = lax.all_gather(output_grads, ("row", "fsdp"), axis=0, tiled=True)
    grad = block_product(lax.all_gather(layer_inputs, "col", axis=0, tiled=True), grads_all)
    keep_elem = expand_keep(tile_keep)
    return adam_update(grad, weight, moment, variance, keep_elem)


def solution(mesh):
    placed = (
        P("col", ("row", "fsdp")),
        P(("row", "fsdp"), "col"),
        P(("row", "fsdp"), "col"),
        P(("row", "fsdp"), "col"),
        P(("row", "fsdp"), "col"),
        P(),
    )
    return jax.shard_map(
        per_device,
        mesh=mesh,
        in_specs=placed,
        out_specs=(P(("row", "fsdp"), "col"), P(("row", "fsdp"), "col"), P(("row", "fsdp"), "col")),
        check_vma=False,
    )
```

profile of v0, /device:TPU:1, one launch (start us, length us, event | category | flops | bytes accessed | tf_op | source)
XLA Modules:
  0.0 235.8 jit_solution(5885897363916849226)
XLA Ops:
  7.2 0.0 all-gather.3.cloned.1.call-start
  7.2 0.7 all-gather.3.cloned.1.call-update
  7.9 0.0 all-gather.5.cloned.1.call-start
  7.9 0.7 all-gather.5.cloned.1.call-update
  8.7 0.8 dynamic-slice_compare_fusion
  9.4 65.5 %all-gather.3.cloned.1.call-done = bf16[4096,256]{1,0:T(8,128)(2,1)} async-done(((bf16[256,256]{1,0:T(8,128)(2,1)}), bf16[4096,256]{1,0:T(8,128)(2,1)}) %all-gather.3.cloned.1.call-update) | async-done | bytes 2097168 | tf_op jit(solution)/shard_map/all_gather | solution.py:58
  75.0 145.1 %all-gather.5.cloned.1.call-done = bf16[4096,896]{1,0:T(8,128)(2,1)} async-done(((bf16[128,896]{1,0:T(8,128)(2,1)}), bf16[4096,896]{1,0:T(8,128)(2,1)}) %all-gather.5.cloned.1.call-update) | async-done | bytes 7340048 | tf_op jit(solution)/shard_map/all_gather | solution.py:57
  220.1 0.1 broadcast_in_dim.2
  220.2 8.8 %bitcast_select_fusion = (bf16[256,896]{1,0:T(8,128)(2,1)}, bf16[256,896]{1,0:T(8,128)(2,1)}, bf16[256,896]{1,0:T(8,128)(2,1)}) fusion(bf16[256,896]{1,0:T(8,128)(2,1)} %param.10, pred[32,8,7,128]{3,2,1,0:T(8,128)(4,1)S(1)} %bitcast.8, bf16[256,896]{1,0:T(8,128)(2,1)} %param.8, bf16[256,896]{1,0:T(8,128)(2,1)} %param.9, ...), kind=kOutput, calls=%fused_computation.8 | convolution fusion | flops 1884553216 | bytes 12419072 | tf_op jit(solution)/shard_map/dot_general | solution.py:23
Async XLA Ops:
  7.2 67.8 %all-gather.3.cloned.1.call-start = ((), (), s32[]{:S(2)}) async-start(), calls=%async_computation | async-start | bytes 2228224 | tf_op jit(solution)/shard_map/all_gather | solution.py:58
  7.9 212.2 %all-gather.5.cloned.1.call-start = ((), (), s32[]{:S(2)}) async-start(), calls=%async_computation.1 | async-start | bytes 7569408 | tf_op jit(solution)/shard_map/all_gather | solution.py:57
Sparse Core Ops, SparseCore 0:
  11.0 63.9 all-gather.2
  77.0 142.9 all-gather.4
where the time goes:
time: 236 us
  waiting for transfers between devices  212 us (90%)
  between operations  14 us (6%)
  matrix products  8.78 us (4%)
    all_gather x1, waiting for transfers between devices, per_device(): lax.all_gather(output_grads, ('row', 'fsdp'), axis=0, tiled=True)  145 us
    all_gather x1, waiting for transfers between devices, per_device(): lax.all_gather(layer_inputs, 'col', axis=0, tiled=True)  65.5 us
    dot_general x1, matrix products, block_product(): lax.dot_general(left_cols, right_cols, (((0,), (0,)), ((), ())), preferre...  8.78 us
  transfers between devices with their start and end apart: 2, of which 2 were waited for; matrix products, arithmetic and copies ran while one was open for 0% of the time, Pallas kernels for 0%

commit v1 on v0

--- a/solution.py
+++ b/solution.py
@@ -55,7 +55,12 @@
         (row_blocks, col_blocks),
     )
     grads_all = lax.all_gather(output_grads, ("row", "fsdp"), axis=0, tiled=True)
-    grad = block_product(lax.all_gather(layer_inputs, "col", axis=0, tiled=True), grads_all)
+    grad = block_product(
+        jnp.concatenate(
+            lax.all_to_all(jnp.stack([layer_inputs] * lax.axis_size("col")), "col", 0, 0), axis=0
+        ),
+        grads_all,
+    )
     keep_elem = expand_keep(tile_keep)
     return adam_update(grad, weight, moment, variance, keep_elem)
 

time: 236 us -> 172 us (0.73)
  waiting for transfers between devices: 212 us -> 139 us
  starting transfers between devices: 0.08 us -> 7.74 us
  local copies, waits for them, and re-layouts: 0.14 us -> 2.65 us
    all_gather x1 -> x0, waiting for transfers between devices: 65.5 us -> none  [per_device(): lax.all_gather(layer_inputs, 'col', axis=0, tiled=True)]
    all_gather x1, waiting for transfers between devices: 145 us -> 114 us  [per_device(): lax.all_gather(output_grads, ('row', 'fsdp'), axis=0, tiled=True)]
    all_to_all x0 -> x1, waiting for transfers between devices: none -> 24.7 us  [per_device(): lax.all_to_all(jnp.stack([layer_inputs] * lax.axis_size('col')), 'col', 0...]
    all_to_all x0 -> x1, starting transfers between devices: none -> 7.7 us  [per_device(): lax.all_to_all(jnp.stack([layer_inputs] * lax.axis_size('col')), 'col', 0...]
    another operation x0 -> x1, local copies, waits for them, and re-layouts: none -> 2.5 us  [per_device(): jnp.stack([layer_inputs] * lax.axis_size('col'))]
  transfers between devices with their start and end apart: 2 -> 2, of which waited for: 2 -> 2; matrix products, arithmetic and copies ran while one was open for 0% -> 2% of each run, Pallas kernels for 0% -> 0%
where the time goes in v1:
time: 172 us
  waiting for transfers between devices  139 us (81%)
  between operations  14.1 us (8%)
  starting transfers between devices  7.74 us (4%)
  matrix products  7.41 us (4%)
  local copies, waits for them, and re-layouts  2.65 us (2%)
    all_gather x1, waiting for transfers between devices, per_device(): lax.all_gather(output_grads, ('row', 'fsdp'), axis=0, tiled=True)  114 us
    all_to_all x1, waiting for transfers between devices, per_device(): lax.all_to_all(jnp.stack([layer_inputs] * lax.axis_size('col')), 'col', 0...  24.7 us
    all_to_all x1, starting transfers between devices, per_device(): lax.all_to_all(jnp.stack([layer_inputs] * lax.axis_size('col')), 'col', 0...  7.7 us
    dot_general x1, matrix products, block_product(): lax.dot_general(left_cols, right_cols, (((0,), (0,)), ((), ())), preferre...  7.41 us
  transfers between devices with their start and end apart: 2, of which 2 were waited for; matrix products, arithmetic and copies ran while one was open for 2% of the time, Pallas kernels for 0%

profile of v1, /device:TPU:1, one launch (start us, length us, event | category | flops | bytes accessed | tf_op | source)
XLA Modules:
  0.0 172.0 jit_solution(15847445086680285053)
XLA Ops:
  7.2 0.0 all-gather.2.cloned.1.call-start
  7.2 0.7 all-gather.2.cloned.1.call-update
  7.9 2.5 %stack.2 = bf16[16,256,256]{2,1,0:T(8,128)(2,1)} broadcast(bf16[256,256]{1,0:T(8,128)(2,1)} %param.6), dimensions={1,2} | broadcast | bytes 2228224 | tf_op jit(solution)/shard_map/stack | solution.py:60
  10.4 0.0 copy-start
  10.4 0.0 copy-start.1
  10.4 0.0 copy-start.2
  10.4 7.7 %all-to-all-start = ((bf16[16,256,256]{2,1,0:T(8,128)(2,1)}), bf16[16,256,256]{2,1,0:T(8,128)(2,1)S(1)}, u32[]{:S(2)}, u32[]{:S(2)}) async-start(bf16[16,256,256]{2,1,0:T(8,128)(2,1)} %stack.2), calls=%async_computation | async-start | bytes 4194304 | tf_op jit(solution)/shard_map/all_to_all | solution.py:60
  18.1 0.8 dynamic-slice_compare_fusion
  18.9 24.7 %all-to-all-done = bf16[16,256,256]{2,1,0:T(8,128)(2,1)S(1)} async-done(((bf16[16,256,256]{2,1,0:T(8,128)(2,1)}), bf16[16,256,256]{2,1,0:T(8,128)(2,1)S(1)}, u32[]{:S(2)}, u32[]{:S(2)}) %all-to-all-start) | async-done | bytes 2097184 | tf_op jit(solution)/shard_map/all_to_all | solution.py:60
  43.6 114.0 %all-gather.2.cloned.1.call-done = bf16[4096,896]{1,0:T(8,128)(2,1)} async-done(((bf16[128,896]{1,0:T(8,128)(2,1)}), bf16[4096,896]{1,0:T(8,128)(2,1)}) %all-gather.2.cloned.1.call-update) | async-done | bytes 7340048 | tf_op jit(solution)/shard_map/all_gather | solution.py:57
  157.6 0.1 broadcast_in_dim.2
  157.7 0.0 copy-done
  157.8 0.0 copy-done.1
  157.8 0.0 copy-done.2
  157.8 7.4 %bitcast_select_fusion = (bf16[256,896]{1,0:T(8,128)(2,1)}, bf16[256,896]{1,0:T(8,128)(2,1)}, bf16[256,896]{1,0:T(8,128)(2,1)}) fusion(bf16[256,896]{1,0:T(8,128)(2,1)S(1)} %copy-done, pred[32,8,7,128]{3,2,1,0:T(8,128)(4,1)S(1)} %bitcast.10, bf16[256,896]{1,0:T(8,128)(2,1)S(1)} %copy-done.1, bf16[256,896]{1,0:T(8,128)(2,1)S(1)} %copy-done.2, ...), kind=kOutput, calls=%fused_computation.8 | convolution fusion | flops 1884553216 | bytes 12419072 | tf_op jit(solution)/shard_map/dot_general | solution.py:23
Async XLA Ops:
  7.2 150.4 %all-gather.2.cloned.1.call-start = ((), (), s32[]{:S(2)}) async-start(), calls=%async_computation.1 | async-start | bytes 7569408 | tf_op jit(solution)/shard_map/all_gather | solution.py:57
  10.4 147.3 %copy-start = (bf16[256,896]{1,0:T(8,128)(2,1)S(1)}, bf16[256,896]{1,0:T(8,128)(2,1)}, u32[]{:S(2)}) copy-start(bf16[256,896]{1,0:T(8,128)(2,1)} %param.10) | copy-start | bytes 1376260
  10.4 147.3 %copy-start.1 = (bf16[256,896]{1,0:T(8,128)(2,1)S(1)}, bf16[256,896]{1,0:T(8,128)(2,1)}, u32[]{:S(2)}) copy-start(bf16[256,896]{1,0:T(8,128)(2,1)} %param.8) | copy-start | bytes 1376260
  10.4 147.4 %copy-start.2 = (bf16[256,896]{1,0:T(8,128)(2,1)S(1)}, bf16[256,896]{1,0:T(8,128)(2,1)}, u32[]{:S(2)}) copy-start(bf16[256,896]{1,0:T(8,128)(2,1)} %param.9) | copy-start | bytes 1376260
  10.4 33.1 %all-to-all-start = ((bf16[16,256,256]{2,1,0:T(8,128)(2,1)}), bf16[16,256,256]{2,1,0:T(8,128)(2,1)S(1)}, u32[]{:S(2)}, u32[]{:S(2)}) async-start(bf16[16,256,256]{2,1,0:T(8,128)(2,1)} %stack.2), calls=%async_computation | async-start | bytes 4194304 | tf_op jit(solution)/shard_map/all_to_all | solution.py:60
Sparse Core Ops, SparseCore 0:
  10.0 147.5 all-gather.1
